TPU v7x, 32 devices: a whole 2x2x4 slice. The times are simulated.
32 devices in a mesh: req: 4 (over y, x), mlp: 8 (over z, core).
Axes of the slice: x: 2, y: 2, z: 4, core: 2. Of those that a mesh axis runs over, the one named last changes fastest.
Arguments:
- tokens: bfloat16 [64, 4608], P(('req', 'mlp')), may hold values from -6 to 6
- segments: int32 [4, 16], replicated, may hold values from 0 to 3, never falling along the last dimension, each value on 1 to 8 neighbouring positions
- owners: int32 [4], replicated, may hold values from 0 to 3, each once
- sink_keys: bfloat16 [4, 2048], P(None, 'mlp'), may hold values from -21 to 21
- sink_values: bfloat16 [4, 2048], P(None, 'mlp'), may hold values from -6 to 6
- window_keys: bfloat16 [4096, 2048], P('req', 'mlp'), may hold values from -6 to 6
- window_values: bfloat16 [4096, 2048], P('req', 'mlp'), may hold values from -6 to 6
- attn_gain: float32 [4608], replicated, may hold values from 0.1 to 1.9
- post_attn_gain: float32 [4608], replicated, may hold values from 0.1 to 1.9
- ffn_gain: float32 [4608], replicated, may hold values from 0.1 to 1.9
- post_ffn_gain: float32 [4608], replicated, may hold values from 0.1 to 1.9
- w_query: bfloat16 [4608, 4096], P(None, 'mlp'), may hold values from -0.09375 to 0.09375
- w_key: bfloat16 [4608, 2048], P(None, 'mlp'), may hold values from -0.25 to 0.25
- w_value: bfloat16 [4608, 2048], P(None, 'mlp'), may hold values from -0.09375 to 0.09375
- w_out: bfloat16 [4096, 4608], P('mlp'), may hold values from -0.09375 to 0.09375
- w_gate: bfloat16 [36864, 4608], P(('req', 'mlp')), may hold values from -0.09375 to 0.09375
- w_up: bfloat16 [36864, 4608], P(('req', 'mlp')), may hold values from -0.09375 to 0.09375
- w_down: bfloat16 [36864, 4608], P(('req', 'mlp')), may hold values from -0.03125 to 0.03125
Outputs:
- mixed: bfloat16 [64, 4608], P(('req', 'mlp'))
Inputs may be any that keep to these rules, and one draw needn't show every extreme that they name: `segments`: row g gives, for the 16 suffix tokens of request group g in order, which of the group's 4 requests each belongs to; a request's tokens are contiguous and its number never falls along the row. Req index d holds array rows d * B to d * B + B - 1 of window_keys and window_values, whose window positions are owners[d] * B to owners[d] * B + B - 1, B = 4096 / 4; every block of positions is held once.
All inputs are finite; a program needn't handle non-finite values.
Results may differ from a plain program's by a relative error of at most 0.015.
Values may be sent and summed in bfloat16 or wider, within the bound.
A program may use at most 128 MiB of HBM per device.

v0:
```python
import jax
import jax.numpy as jnp
from jax import lax
from jax.sharding import PartitionSpec as P

HEADS = 32
KVH = 16
HD = 128
SINK = 4
GTOK = 16


epsilon = 1e-06
soft_cap = 50.0
logit_scale = 1.0 / 12.0


def rms_scale(values):
    return values * lax.rsqrt(jnp.mean(values * values, axis=-1, keepdims=True) + epsilon)


def positions(seg_rows):
    ordering = jnp.arange(seg_rows.shape[-1], dtype=jnp.int32)
    same_seg = seg_rows[..., :, None] == seg_rows[..., None, :]
    earlier = ordering[None, :] < ordering[:, None]
    return jnp.sum((same_seg & earlier).astype(jnp.int32), axis=-1)


def lookup(entries, indices):
    slots = jnp.arange(entries.shape[0], dtype=jnp.int32)
    return jnp.sum(jnp.where(indices[:, None] == slots[None, :], entries[None, :], 0), axis=1)


def attend(query_rows, key_matrix_rows, value_matrix_rows, visible):
    score_matrix = (
        jnp.einsum(
            "woji,roi->wojr", query_rows, key_matrix_rows, preferred_element_type=jnp.float32
        )
        * logit_scale
    )
    weight = jnp.exp(soft_cap * jnp.tanh(score_matrix / soft_cap))
    weight = jnp.where(visible[:, None, None, :], weight, 0.0)
    totals = jnp.sum(weight, axis=-1)
    summed_output = jnp.einsum(
        "xfka,afq->xfkq",
        weight.astype(jnp.bfloat16),
        value_matrix_rows,
        preferred_element_type=jnp.float32,
    )
    return (summed_output, totals)


def shards(
    tokens,
    segments,
    owners,
    sink_keys,
    sink_values,
    window_keys,
    window_values,
    attn_gain,
    post_attn_gain,
    ffn_gain,
    post_ffn_gain,
    w_query,
    w_key,
    w_value,
    w_out,
    w_gate,
    w_up,
    w_down,
):
    per_kv = HEADS // KVH
    local_heads = w_key.shape[1] // HD
    token_float = tokens.astype(jnp.float32)
    normed = (rms_scale(token_float) * attn_gain).astype(jnp.bfloat16)
    group_rows = lax.all_gather(normed, "mlp", axis=0, tiled=True)
    query_rows = (
        jnp.dot(group_rows, w_query, preferred_element_type=jnp.float32)
        .astype(jnp.bfloat16)
        .reshape(GTOK, local_heads, per_kv, HD)
    )
    key_new = (
        jnp.dot(group_rows, w_key, preferred_element_type=jnp.float32)
        .astype(jnp.bfloat16)
        .reshape(GTOK, local_heads, HD)
    )
    value_new = (
        jnp.dot(group_rows, w_value, preferred_element_type=jnp.float32)
        .astype(jnp.bfloat16)
        .reshape(GTOK, local_heads, HD)
    )
    req_index = lax.axis_index("req")
    pos_all = positions(segments)
    pos_row = lax.dynamic_index_in_dim(pos_all, req_index, 0, keepdims=False)
    seg_row = lax.dynamic_index_in_dim(segments, req_index, 0, keepdims=False)
    sink_key = sink_keys.reshape(SINK, local_heads, HD)
    sink_value = sink_values.reshape(SINK, local_heads, HD)
    sink_sum, sink_tot = attend(
        query_rows, sink_key, sink_value, jnp.ones((GTOK, SINK), dtype=jnp.bool_)
    )
    ordering = jnp.arange(GTOK, dtype=jnp.int32)
    local_vis = (seg_row[:, None] == seg_row[None, :]) & (ordering[None, :] <= ordering[:, None])
    loc_sum, loc_tot = attend(query_rows, key_new, value_new, local_vis)
    block_rows = window_keys.shape[0]
    piece_key = lax.all_gather(window_keys, "req", axis=0, tiled=True).reshape(-1, local_heads, HD)
    piece_value = lax.all_gather(window_values, "req", axis=0, tiled=True).reshape(
        -1, local_heads, HD
    )
    row_ids = jnp.arange(piece_key.shape[0], dtype=jnp.int32)
    window_pos = lookup(owners, row_ids // block_rows) * block_rows + row_ids % block_rows
    part_sum, part_tot = attend(
        query_rows, piece_key, piece_value, window_pos[None, :] > pos_row[:, None]
    )
    merged = (sink_sum + part_sum + loc_sum) / (sink_tot + part_tot + loc_tot)[..., None]
    attended = merged.astype(jnp.bfloat16).reshape(GTOK, local_heads * per_kv * HD)
    projected = jnp.dot(attended, w_out, preferred_element_type=jnp.float32)
    head_total = lax.psum_scatter(
        projected.astype(jnp.bfloat16), "mlp", scatter_dimension=0, tiled=True
    ).astype(jnp.float32)
    residual = token_float + rms_scale(head_total) * post_attn_gain
    ffn_in = (rms_scale(residual) * ffn_gain).astype(jnp.bfloat16)
    contract = (((1,), (1,)), ((), ()))
    piece = lax.all_gather(ffn_in, ("req", "mlp"), axis=0, tiled=True)
    gate_part = lax.dot_general(piece, w_gate, contract, preferred_element_type=jnp.float32)
    up_part = lax.dot_general(piece, w_up, contract, preferred_element_type=jnp.float32)
    hidden = (jax.nn.gelu(gate_part, approximate=True) * up_part).astype(jnp.bfloat16)
    ffn_out = lax.psum_scatter(
        jnp.dot(hidden, w_down, preferred_element_type=jnp.float32),
        ("req", "mlp"),
        scatter_dimension=0,
        tiled=True,
    )
    return (residual + rms_scale(ffn_out) * post_ffn_gain).astype(jnp.bfloat16)


def solution(mesh):
    return jax.shard_map(
        shards,
        mesh=mesh,
        in_specs=(
            P(("req", "mlp"), None),
            P(),
            P(),
            P(None, "mlp"),
            P(None, "mlp"),
            P("req", "mlp"),
            P("req", "mlp"),
            P(),
            P(),
            P(),
            P(),
            P(None, "mlp"),
            P(None, "mlp"),
            P(None, "mlp"),
            P("mlp", None),
            P(("req", "mlp"), None),
            P(("req", "mlp"), None),
            P(("req", "mlp"), None),
        ),
        out_specs=P(("req", "mlp"), None),
        check_vma=False,
    )
```

profile of v0, /device:TPU:0, one launch (start us, length us, event | category | flops | bytes accessed | tf_op | source)
XLA Modules:
  0.0 348.4 jit_solution(10756203467283247268)
XLA Ops:
  6.5 0.0 copy-start
  6.5 0.0 all-gather.5.cloned.1.call-start
  6.5 2.2 copy.56
  8.8 0.0 all-gather.5.cloned.1.call-update
  8.8 0.0 all-gather.7.cloned.1.call-start
  8.8 2.0 copy.59
  10.9 0.0 all-gather.7.cloned.1.call-update
  10.9 0.0 all-reduce.5.cloned.1.call-start
  10.9 0.9 fusion.36
  11.8 0.8 fusion.43
  12.7 15.7 %all-gather = bf16[8,2,4608]{2,1,0:T(2,128)(2,1)S(1)} all-gather(bf16[1,2,4608]{2,1,0:T(2,128)(2,1)S(1)} %fusion.43), channel_id=1, replica_groups=mesh['req'=4,'mlp'=8] {'mlp'}, dimensions={0}, use_global_device_ids=true | all-gather | bytes 165888 | tf_op jit(solution)/shard_map/all_gather | solution.py:77
  28.4 0.1 reshape.185
  28.5 0.0 copy-start.7
  28.5 0.0 copy-start.9
  28.5 0.0 copy-start.10
  28.5 3.1 convolution_convert_fusion.1
  31.6 0.0 copy-done
  31.6 0.4 convolution_convert_fusion.2
  32.0 0.0 copy-start.8
  32.0 2.1 convolution_convert_fusion.3
  34.1 0.0 copy-done.7
  34.2 0.2 convert_reduce_fusion
  34.4 0.0 copy-done.9
  34.4 0.1 select_reduce_fusion
  34.5 0.1 fusion.55
  34.6 0.0 copy-done.10
  34.6 0.2 fusion.64
  34.8 0.2 fusion.63
  35.0 0.1 broadcast_compare_fusion
  35.1 12.1 %all-gather.5.cloned.1.call-done = bf16[4096,256]{0,1:T(8,128)(2,1)} async-done(((bf16[1024,256]{0,1:T(8,128)(2,1)}), bf16[4096,256]{0,1:T(8,128)(2,1)}) %all-gather.5.cloned.1.call-update) | async-done | bytes 2097168 | tf_op jit(solution)/shard_map/all_gather | solution.py:106
  47.3 2.3 fusion.65
  49.5 0.0 copy-start.11
  49.6 0.0 copy-start.5
  49.6 0.0 copy-start.6
  49.6 34.9 %all-gather.7.cloned.1.call-done = bf16[4096,256]{0,1:T(8,128)(2,1)} async-done(((bf16[1024,256]{0,1:T(8,128)(2,1)}), bf16[4096,256]{0,1:T(8,128)(2,1)}) %all-gather.7.cloned.1.call-update) | async-done | bytes 2097168 | tf_op jit(solution)/shard_map/all_gather | solution.py:107
  84.4 2.4 fusion.20
  86.8 0.0 copy-done.8
  86.9 0.2 fusion.13
  87.1 0.2 fusion.14
  87.3 3.7 %convolution_convert_fusion = bf16[16,4608]{1,0:T(8,128)(2,1)} fusion(bf16[16,512]{1,0:T(8,128)(2,1)S(1)} %reshape.183, bf16[512,4608]{1,0:T(8,128)(2,1)} %param.32), kind=kOutput, calls=%fused_computation | convolution fusion | flops 75571200 | bytes 4882432 | tf_op jit(solution)/shard_map/dot_general | solution.py:117
  91.0 0.0 all-reduce.5.cloned.1.call-update
  91.0 0.0 all-reduce.7.cloned.1.call-start
  91.1 0.0 copy-done.11
  91.1 0.6 dynamic-slice
  92.3 51.0 %all-reduce.5.cloned.1.call-done = bf16[16,4608]{1,0:T(8,128)(2,1)} async-done(((bf16[16,4608]{1,0:T(8,128)(2,1)}), bf16[16,4608]{1,0:T(8,128)(2,1)}) %all-reduce.5.cloned.1.call-update) | async-done | bytes 147472
  143.3 1.0 fusion.34
  144.3 0.0 copy-done.3
  144.3 0.0 copy-done.5
  144.4 1.1 multiply_reduce_fusion.1
  145.5 0.0 copy-done.6
  145.5 0.1 fusion.44
  145.6 0.5 copy-done.1
  146.1 44.4 %all-gather.1 = bf16[32,2,4608]{2,1,0:T(2,128)(2,1)S(1)} all-gather(bf16[1,2,4608]{2,1,0:T(2,128)(2,1)S(1)} %fusion.44), channel_id=1, replica_groups=mesh['req'=4,'mlp'=8] {'req','mlp'}, dimensions={0}, use_global_device_ids=true | all-gather | bytes 608256 | tf_op jit(solution)/shard_map/all_gather | solution.py:124
  190.5 0.2 reshape.187
  190.7 7.3 %fusion.66 = f32[64,1152]{1,0:T(8,128)S(1)} fusion(bf16[64,4608]{1,0:T(8,128)(2,1)S(1)} %reshape.187, bf16[1152,4608]{1,0:T(8,128)(2,1)} %param.33), kind=kOutput, calls=%fused_computation.102 | convolution fusion | flops 679477248 | bytes 11501568 | tf_op jit(solution)/shard_map/dot_general | solution.py:125
  198.0 0.0 copy-start.2
  198.0 0.0 copy-start.4
  198.1 13.6 %fusion.19 = f32[64,4608]{1,0:T(8,128)} fusion(bf16[1152,4608]{1,0:T(8,128)(2,1)} %param.35, bf16[64,4608]{1,0:T(8,128)(2,1)S(1)} %reshape.187, bf16[1152,4608]{1,0:T(8,128)(2,1)} %param.34, f32[64,1152]{1,0:T(8,128)S(1)} %fusion.66), kind=kOutput, calls=%fused_computation.29 | convolution fusion | flops 1359691776 | bytes 23298048 | tf_op jit(solution)/shard_map/dot_general | solution.py:129
  211.7 0.0 all-reduce.7.cloned.1.call-update
  211.7 127.5 %all-reduce.7.cloned.1.call-done = f32[64,4608]{1,0:T(8,128)} async-done(((f32[64,4608]{1,0:T(8,128)}), f32[64,4608]{1,0:T(8,128)}) %all-reduce.7.cloned.1.call-update) | async-done | bytes 1179664
  339.2 1.1 multiply_reduce_fusion
  340.2 0.0 copy-done.2
  340.2 0.0 copy-done.4
  340.3 1.6 add_convert_fusion
  (17 shorter events, 0.2 us)
Async XLA Ops:
  6.5 25.0 %copy-start = (bf16[4608,256]{1,0:T(8,128)(2,1)S(1)}, bf16[4608,256]{1,0:T(8,128)(2,1)}, u32[]{:S(2)}) copy-start(bf16[4608,256]{1,0:T(8,128)(2,1)} %param.30) | copy-start | bytes 7077892
  6.5 40.7 %all-gather.5.cloned.1.call-start = ((), (), s32[]{:S(2)}) async-start(), calls=%async_computation | async-start | bytes 2621440 | tf_op jit(solution)/shard_map/all_gather | solution.py:106
  8.8 75.7 %all-gather.7.cloned.1.call-start = ((), (), s32[]{:S(2)}) async-start(), calls=%async_computation.1 | async-start | bytes 2621440 | tf_op jit(solution)/shard_map/all_gather | solution.py:107
  10.9 132.4 %all-reduce.5.cloned.1.call-start = ((), (), s32[]{:S(2)}) async-start(), calls=%async_computation.2 | async-start | bytes 294912
  28.5 5.7 %copy-start.7 = (s32[4,16]{1,0:T(4,128)S(1)}, s32[4,16]{1,0:T(4,128)}, u32[]{:S(2)}) copy-start(s32[4,16]{1,0:T(4,128)} %param.19) | copy-start | bytes 772
  28.5 5.9 %copy-start.9 = (s32[4]{0:T(128)S(1)}, s32[4]{0:T(128)}, u32[]{:S(2)}) copy-start(s32[4]{0:T(128)} %param.20) | copy-start | bytes 52
  28.5 6.1 %copy-start.10 = (bf16[4,256]{1,0:T(4,128)(2,1)S(1)}, bf16[4,256]{1,0:T(4,128)(2,1)}, u32[]{:S(2)}) copy-start(bf16[4,256]{1,0:T(4,128)(2,1)} %param.21) | copy-start | bytes 6148
  32.0 54.9 %copy-start.8 = (bf16[4,256]{1,0:T(4,128)(2,1)S(1)}, bf16[4,256]{1,0:T(4,128)(2,1)}, u32[]{:S(2)}) copy-start(bf16[4,256]{1,0:T(4,128)(2,1)} %param.22) | copy-start | bytes 6148
  49.5 41.5 %copy-start.11 = (u32[32]{0:T(128)S(1)}, u32[32]{0:T(128)}, u32[]{:S(2)}) copy-start(u32[32]{0:T(128)} %constant.81) | copy-start | bytes 388
  49.6 94.8 %copy-start.3 = (bf16[2,4608]{1,0:T(2,128)(2,1)S(1)}, bf16[2,4608]{1,0:T(2,128)(2,1)}, u32[]{:S(2)}) copy-start(bf16[2,4608]{1,0:T(2,128)(2,1)} %param.18) | copy-start | bytes 55300
  49.6 94.8 %copy-start.5 = (f32[4608]{0:T(1024)S(1)}, f32[4608]{0:T(1024)}, u32[]{:S(2)}) copy-start(f32[4608]{0:T(1024)} %param.26) | copy-start | bytes 55300
  49.6 95.9 %copy-start.6 = (f32[4608]{0:T(1024)S(1)}, f32[4608]{0:T(1024)}, u32[]{:S(2)}) copy-start(f32[4608]{0:T(1024)} %param.27) | copy-start | bytes 55300
  91.0 248.1 %all-reduce.7.cloned.1.call-start = ((), (), s32[]{:S(2)}) async-start(), calls=%async_computation.3 | async-start | bytes 2359296
  145.5 0.6 copy-start.1
  198.0 142.2 %copy-start.2 = (f32[2,4608]{1,0:T(2,128)S(1)}, f32[2,4608]{1,0:T(2,128)}, u32[]{:S(2)}) copy-start(f32[2,4608]{1,0:T(2,128)} %copy-done.1) | copy-start | bytes 110596
  198.0 142.2 %copy-start.4 = (f32[4608]{0:T(1024)S(1)}, f32[4608]{0:T(1024)}, u32[]{:S(2)}) copy-start(f32[4608]{0:T(1024)} %param.28) | copy-start | bytes 55300
Sparse Core Ops, SparseCore 0:
  9.2 38.0 all-gather.4
  49.1 35.2 all-gather.6
  91.2 52.0 all-reduce.4
  211.8 127.3 all-reduce.6
where the time goes:
time: 349 us; the launch traced here: 348 us
  waiting for transfers between devices  225 us (64%)
  blocking collectives  60.1 us (17%)
  matrix products  35.6 us (10%)
  between operations  14 us (4%)
  other arithmetic  7.19 us (2%)
  local copies, waits for them, and re-layouts  5.76 us (2%)
    unnamed x6, waiting for transfers between devices  178 us
    all_gather x1, blocking collectives, shards(): piece = lax.all_gather(ffn_in, ('req', 'mlp'), axis=0, tiled=True)  44.4 us
    all_gather x1, waiting for transfers between devices, shards(): lax.all_gather(window_values, 'req', axis=0, tiled=True)  34.9 us
    all_gather x1, blocking collectives, shards(): group_rows = lax.all_gather(normed, 'mlp', axis=0, tiled=True)  15.7 us
    dot_general x1, matrix products, shards(): jnp.dot(hidden, w_down, preferred_element_type=jnp.float32)  13.6 us
    all_gather x1, waiting for transfers between devices, shards(): lax.all_gather(window_keys, 'req', axis=0, tiled=True)  12.1 us
    dot_general x1, matrix products, shards(): lax.dot_general(piece, w_gate, contract, preferred_element_type=jnp.float32)  7.31 us
  transfers between devices with their start and end apart: 4, of which 4 were waited for; matrix products, arithmetic and copies ran while one was open for 4% of the time, Pallas kernels for 0%

commit v1 on v0

v1 whole, which is shorter than its diff:
```python
import functools
import math

import jax
import jax.numpy as jnp
from jax import lax
from jax.experimental import pallas as pl
from jax.experimental.pallas import tpu as pltpu
from jax.sharding import PartitionSpec as P

HD = 128
EPS = 1e-06
SOFT_CAP = 50.0
SCORE_SCALE = 1.0 / (12.0 * SOFT_CAP)
MESH = pl.DeviceIdType.MESH
F32 = jnp.float32
BF16 = jnp.bfloat16
NT = (((1,), (1,)), ((), ()))
GELU_C = math.sqrt(2.0 / math.pi)


def rms_scale(values):
    return values * lax.rsqrt(jnp.mean(values * values, axis=-1, keepdims=True) + EPS)


def weights_of(scores):
    return jnp.exp(SOFT_CAP * jnp.tanh(scores * SCORE_SCALE))


def chunks(total, size):
    return [(start, min(size, total - start)) for start in range(0, total, size)]


def kernel(
    n_req, n_mlp,
    tok, attn_gain, post_attn_gain, ffn_gain, post_ffn_gain, wpos, pos, emask, sink_k, sink_v,
    wk_hbm, wv_hbm, wq_hbm, wkey_hbm, wval_hbm, wo_hbm, wg_hbm, wu_hbm, wd_hbm,
    out,
    win_k, win_v, wq, wkey, wval, wo, wg, wu, wd, load_sem,
    ag1, xf, xb, qbuf, ekf, evf, psend, prec,
    pj, s1, r1, s3, r3,
    ag2, hid, acc,
    t1, u1, t2, u2, t3f, t3, u3,
    ss_ag1z, rs_ag1z, ss_ag1c, rs_ag1c, ss_q, rs_q, ss_p, rs_p,
    ss_1, rs_1, ss_3, rs_3,
    ss_ag2z, rs_ag2z, ss_ag2r, rs_ag2r, ss_ag2c, rs_ag2c,
    ss_t1, rs_t1, ss_t2, rs_t2, ss_t3, rs_t3,
):
    n_z = n_mlp // 2
    rq = lax.axis_index("req")
    me = lax.axis_index("mlp")
    z = me // 2
    c = me % 2
    oc = 1 - c
    sib = z * 2 + oc
    tp, width = tok.shape
    group = tp * n_mlp
    total = group * n_req
    kv_cols = wkey.shape[1]
    q_cols = wq.shape[1]
    kv_heads = kv_cols // HD
    ff = wg.shape[0]

    def z_peer(step):
        return {"mlp": lax.rem(z + step, n_z) * 2 + c}

    def r_peer(step):
        return lax.rem(rq + step, n_req)

    loads = {}
    for number, (name, src, dst) in enumerate((
        ("q", wq_hbm, wq), ("k", wkey_hbm, wkey), ("v", wval_hbm, wval),
        ("wk", wk_hbm, win_k), ("wv", wv_hbm, win_v), ("o", wo_hbm, wo),
        ("g", wg_hbm, wg), ("u", wu_hbm, wu), ("d", wd_hbm, wd),
    )):
        loads[name] = pltpu.make_async_copy(src, dst, load_sem.at[number])
        loads[name].start()

    barrier = pltpu.get_barrier_semaphore()
    pl.semaphore_signal(barrier, inc=1, device_id={"mlp": sib}, device_id_type=MESH)
    for step in range(1, n_z):
        pl.semaphore_signal(barrier, inc=1, device_id=z_peer(step), device_id_type=MESH)
    for step in range(1, n_req):
        pl.semaphore_signal(barrier, inc=1, device_id={"req": r_peer(step)}, device_id_type=MESH)

    sent = []

    def send(src, dst, send_sem, recv_sem, device):
        copy = pltpu.make_async_remote_copy(
            src_ref=src, dst_ref=dst, send_sem=send_sem, recv_sem=recv_sem,
            device_id=device, device_id_type=MESH,
        )
        copy.start()
        sent.append(copy)
        return copy

    token_float = tok[...].astype(F32)
    ag1[c, z] = (rms_scale(token_float) * attn_gain[...]).astype(BF16)
    pl.semaphore_wait(barrier, n_z + n_req - 1)
    z_copies = [
        send(ag1.at[c, z], ag1.at[c, z], ss_ag1z.at[k], rs_ag1z.at[k], z_peer(k))
        for k in range(1, n_z)
    ]
    c_copies = [send(ag1.at[c, z], ag1.at[c, z], ss_ag1c.at[0], rs_ag1c.at[0], {"mlp": sib})]
    for k, copy in enumerate(z_copies, 1):
        copy.wait_recv()
        block = ag1.at[c, lax.rem(z + n_z - k, n_z)]
        c_copies.append(send(block, block, ss_ag1c.at[k], rs_ag1c.at[k], {"mlp": sib}))
    for copy in c_copies:
        copy.wait_recv()
    for core in range(2):
        for level in range(n_z):
            row = (level * 2 + core) * tp
            xf[row:row + tp, :] = ag1[core, level].astype(F32)
    rows = xf[0:group, :].astype(BF16)

    loads["q"].wait()
    qbuf[rq] = jnp.dot(rows, wq[...], preferred_element_type=F32).astype(BF16)
    q_copies = [
        send(qbuf.at[rq], qbuf.at[rq], ss_q.at[k], rs_q.at[k], {"req": r_peer(k)})
        for k in range(1, n_req)
    ]
    loads["k"].wait()
    key_new = jnp.dot(rows, wkey[...], preferred_element_type=F32).astype(BF16)
    loads["v"].wait()
    value_new = jnp.dot(rows, wval[...], preferred_element_type=F32).astype(BF16)
    n_sink = sink_k.shape[0]
    for target, new, sinks in ((ekf, key_new, sink_k), (evf, value_new, sink_v)):
        target[...] = jnp.zeros_like(target)
        target[0:group, :] = new.astype(F32)
        target[group:group + n_sink, :] = sinks[...].astype(F32)

    own_q = qbuf[rq]
    extra_k = ekf[...].astype(BF16)
    extra_v = evf[...].astype(BF16)
    own_num, own_den = [], []
    for j in range(kv_heads):
        lanes = slice(j * HD, (j + 1) * HD)
        pair = jnp.concatenate(
            [own_q[:, (2 * j + i) * HD:(2 * j + i + 1) * HD] for i in range(2)], axis=0)
        scores = lax.dot_general(pair, extra_k[:, lanes], NT, preferred_element_type=F32)
        weight = jnp.where(emask[...] > 0, weights_of(scores), 0.0)
        den = jnp.sum(weight, axis=-1, keepdims=True)
        num = jnp.dot(weight.astype(BF16), extra_v[:, lanes], preferred_element_type=F32)
        for i in range(2):
            own_num.append(num[i * group:(i + 1) * group])
            own_den.append(den[i * group:(i + 1) * group])

    loads["wk"].wait()
    loads["wv"].wait()
    for copy in q_copies:
        copy.wait_recv()
    all_q = qbuf[...].reshape(total, q_cols)
    visible = wpos[...] > pos[...]
    lane = lax.broadcasted_iota(jnp.int32, (total, HD), 1)
    den_all = jnp.zeros((total, HD), F32)
    for j in range(kv_heads):
        lanes = slice(j * HD, (j + 1) * HD)
        pair = jnp.concatenate(
            [all_q[:, (2 * j + i) * HD:(2 * j + i + 1) * HD] for i in range(2)], axis=0)
        scores = lax.dot_general(pair, win_k[:, lanes], NT, preferred_element_type=F32)
        weight = jnp.where(visible, weights_of(scores), 0.0)
        den = jnp.sum(weight, axis=-1, keepdims=True)
        num = jnp.dot(weight.astype(BF16), win_v[:, lanes], preferred_element_type=F32)
        for i in range(2):
            h = 2 * j + i
            psend[:, :, h * HD:(h + 1) * HD] = num[i * total:(i + 1) * total].reshape(n_req, group, HD)
            den_all = jnp.where(lane == h, den[i * total:(i + 1) * total], den_all)
    psend[:, :, q_cols:q_cols + HD] = den_all.reshape(n_req, group, HD)
    p_copies = [
        send(psend.at[r_peer(k)], prec.at[k - 1], ss_p.at[k], rs_p.at[k], {"req": r_peer(k)})
        for k in range(1, n_req)
    ]
    partial = psend[rq]
    for k, copy in enumerate(p_copies, 1):
        copy.wait_recv()
        partial = partial + prec[k - 1]
    heads = []
    for h in range(2 * kv_heads):
        num = own_num[h] + partial[:, h * HD:(h + 1) * HD]
        den = own_den[h] + partial[:, q_cols + h:q_cols + h + 1]
        heads.append((num / den).astype(BF16))
    attended = jnp.concatenate(heads, axis=1)
    loads["o"].wait()
    for start, size in chunks(width, 512):
        pj[:, start:start + size] = jnp.dot(
            attended, wo[:, start:start + size], preferred_element_type=F32)

    for core in range(2):
        for level in range(n_z):
            row = (level * 2 + core) * tp
            s1[core, level] = pj[row:row + tp, :].astype(BF16)
    send(s1.at[oc], r1, ss_1, rs_1, {"mlp": sib}).wait_recv()
    for level in range(n_z):
        s3[level] = (s1[c, level].astype(F32) + r1[level].astype(F32)).astype(BF16)
    copies = [
        send(s3.at[lax.rem(z + k, n_z)], r3.at[k - 1], ss_3.at[k], rs_3.at[k], z_peer(k))
        for k in range(1, n_z)
    ]
    head_total = s1[c, z].astype(F32) + r1[z].astype(F32)
    for k, copy in enumerate(copies, 1):
        copy.wait_recv()
        head_total = head_total + r3[k - 1].astype(F32)
    residual = token_float + rms_scale(head_total) * post_attn_gain[...]

    mine = c * n_req + rq
    ag2[mine, z] = (rms_scale(residual) * ffn_gain[...]).astype(BF16)
    copies = [
        send(ag2.at[mine, z], ag2.at[mine, z], ss_ag2z.at[k], rs_ag2z.at[k], z_peer(k))
        for k in range(1, n_z)
    ]
    for copy in copies:
        copy.wait_recv()
    r_copies = [
        send(ag2.at[mine], ag2.at[mine], ss_ag2r.at[k], rs_ag2r.at[k], {"req": r_peer(k)})
        for k in range(1, n_req)
    ]
    c_copies = [send(ag2.at[mine], ag2.at[mine], ss_ag2c.at[0], rs_ag2c.at[0], {"mlp": sib})]
    for k, copy in enumerate(r_copies, 1):
        copy.wait_recv()
        block = ag2.at[c * n_req + lax.rem(rq + n_req - k, n_req)]
        c_copies.append(send(block, block, ss_ag2c.at[k], rs_ag2c.at[k], {"mlp": sib}))
    for copy in c_copies:
        copy.wait_recv()
    for core in range(2):
        for r in range(n_req):
            for level in range(n_z):
                row = r * group + (level * 2 + core) * tp
                xf[row:row + tp, :] = ag2[core * n_req + r, level].astype(F32)
    xb[...] = xf[...].astype(BF16)

    loads["g"].wait()
    loads["u"].wait()

    def ffn_hidden(start, size):
        gate = lax.dot_general(
            xb[...], wg[pl.ds(start, size), :], NT, preferred_element_type=F32)
        up = lax.dot_general(
            xb[...], wu[pl.ds(start, size), :], NT, preferred_element_type=F32)
        inner = GELU_C * (gate + 0.044715 * (gate * gate * gate))
        hid[:, pl.ds(start, size)] = (0.5 * gate * (1.0 + jnp.tanh(inner)) * up).astype(BF16)

    if ff >= 256:
        @pl.loop(0, ff // 256)
        def _(step):
            ffn_hidden(pl.multiple_of(step * 256, 256), 256)
    if ff % 256:
        ffn_hidden(ff - ff % 256, ff % 256)
    loads["d"].wait()

    @pl.loop(0, width // 512)
    def _(step):
        lanes = pl.ds(pl.multiple_of(step * 512, 512), 512)
        acc[:, lanes] = jnp.dot(hid[...], wd[:, lanes], preferred_element_type=F32)

    for core in range(2):
        for r in range(n_req):
            for level in range(n_z):
                row = r * group + (level * 2 + core) * tp
                t1[core, r, level] = acc[row:row + tp, :].astype(BF16)
    order = [r_peer(k) for k in list(range(1, n_req)) + [0]]
    first = [
        send(t1.at[oc, r], u1.at[r], ss_t1.at[k], rs_t1.at[k], {"mlp": sib})
        for k, r in enumerate(order)
    ]
    second = []
    for k, r in enumerate(order):
        first[k].wait_recv()
        both = t1[c, r].astype(F32) + u1[r].astype(F32)
        if k < n_req - 1:
            t2[r] = both.astype(BF16)
            second.append(send(
                t2.at[r], u2.at[k], ss_t2.at[k], rs_t2.at[k], {"req": r}))
    for k, copy in enumerate(second):
        copy.wait_recv()
        both = both + u2[k].astype(F32)
    t3f[...] = both
    t3[...] = both.astype(BF16)
    copies = [
        send(t3.at[lax.rem(z + k, n_z)], u3.at[k - 1], ss_t3.at[k], rs_t3.at[k], z_peer(k))
        for k in range(1, n_z)
    ]
    ffn_out = t3f[z]
    for k, copy in enumerate(copies, 1):
        copy.wait_recv()
        ffn_out = ffn_out + u3[k - 1].astype(F32)
    out[...] = (residual + rms_scale(ffn_out) * post_ffn_gain[...]).astype(BF16)
    for copy in sent:
        copy.wait_send()


def positions(seg_rows):
    ordering = jnp.arange(seg_rows.shape[-1], dtype=jnp.int32)
    same_seg = seg_rows[..., :, None] == seg_rows[..., None, :]
    earlier = ordering[None, :] < ordering[:, None]
    return jnp.sum((same_seg & earlier).astype(jnp.int32), axis=-1)


def shards(
    n_req, n_mlp,
    tokens, segments, owners, sink_keys, sink_values, window_keys, window_values,
    attn_gain, post_attn_gain, ffn_gain, post_ffn_gain,
    w_query, w_key, w_value, w_out, w_gate, w_up, w_down,
):
    tp, width = tokens.shape
    n_z = n_mlp // 2
    group = tp * n_mlp
    total = group * n_req
    block = window_keys.shape[0]
    q_cols, kv_cols, ff = w_query.shape[1], w_key.shape[1], w_gate.shape[0]
    n_sink = sink_keys.shape[0]
    extra = 2 * group
    req = lax.axis_index("req")
    pos = positions(segments).reshape(total, 1)
    pos = jnp.concatenate([pos, pos], axis=0)
    owner = jnp.sum(jnp.where(jnp.arange(n_req) == req, owners, 0))
    wpos = (owner * block + jnp.arange(block, dtype=jnp.int32)).reshape(1, block)
    seg = lax.dynamic_index_in_dim(segments, req, 0, keepdims=False)
    order = jnp.arange(group, dtype=jnp.int32)
    local = (seg[:, None] == seg[None, :]) & (order[None, :] <= order[:, None])
    sinks = jnp.broadcast_to(jnp.arange(extra - group) < n_sink, (group, extra - group))
    emask = jnp.concatenate([local, sinks], axis=1).astype(jnp.int32)
    emask = jnp.concatenate([emask, emask], axis=0)

    def v(shape, dtype=BF16):
        return pltpu.VMEM(shape, dtype)

    dma = pltpu.SemaphoreType.DMA
    scratch = [v(a.shape) for a in (
        window_keys, window_values, w_query, w_key, w_value, w_out, w_gate, w_up, w_down)]
    scratch += [
        dma((9,)),
        v((2, n_z, tp, width)), v((total, width), F32), v((total, width)),
        v((n_req, group, q_cols)), v((extra, kv_cols), F32), v((extra, kv_cols), F32),
        v((n_req, group, q_cols + HD), F32), v((max(n_req - 1, 1), group, q_cols + HD), F32),
        v((group, width), F32), v((2, n_z, tp, width)), v((n_z, tp, width)),
        v((n_z, tp, width)), v((n_z - 1, tp, width)),
        v((2 * n_req, n_z, tp, width)), v((total, ff)), v((total, width), F32),
        v((2, n_req, n_z, tp, width)), v((n_req, n_z, tp, width)),
        v((n_req, n_z, tp, width)), v((n_req - 1, n_z, tp, width)),
        v((n_z, tp, width), F32), v((n_z, tp, width)), v((n_z - 1, tp, width)),
        dma((n_z,)), dma((n_z,)), dma((n_z,)), dma((n_z,)),
        dma((n_req,)), dma((n_req,)), dma((n_req,)), dma((n_req,)),
        dma, dma, dma((n_z,)), dma((n_z,)),
        dma((n_z,)), dma((n_z,)), dma((n_req,)), dma((n_req,)), dma((n_req,)), dma((n_req,)),
        dma((n_req,)), dma((n_req,)), dma((n_req,)), dma((n_req,)), dma((n_z,)), dma((n_z,)),
    ]
    vmem = pl.BlockSpec(memory_space=pltpu.VMEM)
    hbm = pl.BlockSpec(memory_space=pl.ANY)
    return pl.pallas_call(
        functools.partial(kernel, n_req, n_mlp),
        name="layer",
        out_shape=jax.ShapeDtypeStruct((tp, width), BF16),
        in_specs=[vmem] * 10 + [hbm] * 9,
        out_specs=vmem,
        scratch_shapes=scratch,
        compiler_params=pltpu.CompilerParams(
            collective_id=0, has_side_effects=True, vmem_limit_bytes=62 << 20),
    )(
        tokens, attn_gain[None], post_attn_gain[None], ffn_gain[None], post_ffn_gain[None],
        wpos, pos, emask, sink_keys, sink_values,
        window_keys, window_values, w_query, w_key, w_value, w_out, w_gate, w_up, w_down,
    )


def solution(mesh):
    both = P(("req", "mlp"), None)
    return jax.shard_map(
        functools.partial(shards, mesh.shape["req"], mesh.shape["mlp"]),
        mesh=mesh,
        in_specs=(
            both, P(), P(), P(None, "mlp"), P(None, "mlp"), P("req", "mlp"), P("req", "mlp"),
            P(), P(), P(), P(),
            P(None, "mlp"), P(None, "mlp"), P(None, "mlp"), P("mlp", None), both, both, both,
        ),
        out_specs=both,
        check_vma=False,
    )
```

time: 349 us -> 69.8 us (0.20)
  waiting for transfers between devices: 225 us -> 0 us
  blocking collectives: 60.1 us -> 0 us
  Pallas kernels: 0 us -> 56.7 us
  matrix products: 35.6 us -> 0 us
  between operations: 14 us -> 0.68 us
  other arithmetic: 7.19 us -> 3.7 us
    unnamed x6 -> x0, waiting for transfers between devices: 178 us -> none
    all_gather x2 -> x0, blocking collectives: 60.1 us -> none  [the longest x1 44.4 us: shards(): piece = lax.all_gather(ffn_in, ('req', 'mlp'), axis=0, tiled=True)]
    pallas_call x0 -> x1, Pallas kernels: none -> 56.7 us  [shards(): pl.pallas_call(functools.partial(kernel, n_req, n_mlp), name='layer', out...]
    all_gather x2 -> x0, waiting for transfers between devices: 47 us -> none  [the longest x1 34.9 us: shards(): lax.all_gather(window_values, 'req', axis=0, tiled=True)]
    dot_general x12 -> x0, matrix products: 35.6 us -> none  [the longest x1 13.6 us: shards(): jnp.dot(hidden, w_down, preferred_element_type=jnp.float32)]
    broadcast_in_dim x0 -> x5, local copies, waits for them, and re-layouts: none -> 5.36 us  [the longest x1 1.35 us: shards(): attn_gain[None]]
    unnamed x29 -> x1, local copies, waits for them, and re-layouts: 5.67 us -> 1.34 us
  transfers between devices with their start and end apart: 4 -> 0, of which waited for: 4 -> 0; matrix products, arithmetic and copies ran while one was open for 4% -> 0% of each run, Pallas kernels for 0% -> 0%
where the time goes in v1:
time: 69.8 us; the launch traced here: 69.3 us
  Pallas kernels  56.7 us (81%)
  local copies, waits for them, and re-layouts  8.2 us (12%)
  other arithmetic  3.7 us (5%)
    pallas_call x1, Pallas kernels, shards(): pl.pallas_call(functools.partial(kernel, n_req, n_mlp), name='layer', out...  56.7 us

profile of v1, /device:TPU:0, one launch (start us, length us, event | category | flops | bytes accessed | tf_op | source)
XLA Modules:
  0.0 69.3 jit_solution(1936800296111881975)
XLA Ops:
  0.0 0.7 dynamic-slice_bitcast_fusion
  0.7 1.3 %fusion.1 = s32[]{:T(128)} fusion(s32[4]{0:T(128)} %param.20, s32[]{:T(128)S(6)} %axis_index.15), kind=kLoop, calls=%fused_computation.7 | loop fusion | flops 11 | bytes 24 | tf_op jit(solution)/shard_map/reduce_sum | solution.py:316
  2.7 0.1 fusion
  2.7 1.0 %convert_reduce_fusion = s32[4,16]{1,0:T(4,128)S(1)} fusion(s32[4,16]{1,0:T(4,128)} %param.19, pred[16,16]{1,0:T(8,128)(4,1)S(1)} %iota_compare_fusion.1), kind=kLoop, calls=%fused_computation | loop fusion | flops 4032 | bytes 768 | tf_op jit(solution)/shard_map/reduce_sum | solution.py:296
  3.7 0.1 reshape.27
  3.8 0.1 pad_add_fusion
  3.9 0.6 iota_add_fusion.wpos
  4.5 0.7 add_convert_fusion.emask
  5.2 1.3 %broadcast_in_dim.14.attn_gain = f32[1,4608]{1,0:T(1,128)} reshape(f32[4608]{0:T(1024)} %param.25) | data formatting | bytes 36864 | tf_op jit(solution)/shard_map/broadcast_in_dim | solution.py:360
  6.5 1.3 %broadcast_in_dim.15.post_attn_gain = f32[1,4608]{1,0:T(1,128)} reshape(f32[4608]{0:T(1024)} %param.26) | data formatting | bytes 36864 | tf_op jit(solution)/shard_map/broadcast_in_dim | solution.py:360
  7.8 1.3 %broadcast_in_dim.30.ffn_gain = f32[1,4608]{1,0:T(1,128)} reshape(f32[4608]{0:T(1024)} %param.27) | data formatting | bytes 36864 | tf_op jit(solution)/shard_map/broadcast_in_dim | solution.py:360
  9.2 1.3 %broadcast_in_dim.31.post_ffn_gain = f32[1,4608]{1,0:T(1,128)} reshape(f32[4608]{0:T(1024)} %param.28) | data formatting | bytes 36864 | tf_op jit(solution)/shard_map/broadcast_in_dim | solution.py:360
  10.5 0.7 %copy.22.pos = s32[128,1]{1,0:T(8,128)} copy(s32[128,1]{0,1:T(1,128)S(1)} %pad_add_fusion) | data formatting | bytes 1024 | tf_op jit(solution)/shard_map/concatenate | solution.py:315
  11.2 56.7 %layer.1 = bf16[2,4608]{1,0:T(2,128)(2,1)} custom-call(bf16[2,4608]{1,0:T(2,128)(2,1)} %tok.1, f32[1,4608]{1,0:T(1,128)} %broadcast_in_dim.14.attn_gain, f32[1,4608]{1,0:T(1,128)} %broadcast_in_dim.15.post_attn_gain, f32[1,4608]{1,0:T(1,128)} %broadcast_in_dim.30.ffn_gain, f32[1,4608]{1,0:T(1,128)} %broadcast_in_dim.31.post_ffn_gain, ...), custom_call_target="tpu_custom_call" | custom-call | tf_op jit(solution)/shard_map/layer/pallas_call | solution.py:350
  68.0 1.3 %copy.24 = bf16[2,4608]{1,0:T(2,128)(2,1)} copy(bf16[2,4608]{1,0:T(2,128)(2,1)} %layer.1) | data formatting | bytes 36864
  (3 shorter events, 0.0 us)

commit v2 on v1

--- a/solution.py
+++ b/solution.py
@@ -33,10 +33,12 @@
 
 def kernel(
     n_req, n_mlp,
-    tok, attn_gain, post_attn_gain, ffn_gain, post_ffn_gain, wpos, pos, emask, sink_k, sink_v,
+    tok, segments, owners, sink_k, sink_v, gains_a, gains_pa, gains_f, gains_pf,
     wk_hbm, wv_hbm, wq_hbm, wkey_hbm, wval_hbm, wo_hbm, wg_hbm, wu_hbm, wd_hbm,
     out,
-    win_k, win_v, wq, wkey, wval, wo, wg, wu, wd, load_sem,
+    win_k, win_v, wq, wkey, wval, wo, wg, wu, wd,
+    attn_gain, post_attn_gain, ffn_gain, post_ffn_gain, load_sem,
+    posv, segv,
     ag1, xf, xb, qbuf, ekf, evf, psend, prec,
     pj, s1, r1, s3, r3,
     ag2, hid, acc,
@@ -69,12 +71,15 @@
 
     loads = {}
     for number, (name, src, dst) in enumerate((
+        ("ga", gains_a, attn_gain.at[0]), ("gpa", gains_pa, post_attn_gain.at[0]),
+        ("gf", gains_f, ffn_gain.at[0]), ("gpf", gains_pf, post_ffn_gain.at[0]),
         ("q", wq_hbm, wq), ("k", wkey_hbm, wkey), ("v", wval_hbm, wval),
         ("wk", wk_hbm, win_k), ("wv", wv_hbm, win_v), ("o", wo_hbm, wo),
         ("g", wg_hbm, wg), ("u", wu_hbm, wu), ("d", wd_hbm, wd),
     )):
         loads[name] = pltpu.make_async_copy(src, dst, load_sem.at[number])
-        loads[name].start()
+        if name not in ("g", "u", "d"):
+            loads[name].start()
 
     barrier = pltpu.get_barrier_semaphore()
     pl.semaphore_signal(barrier, inc=1, device_id={"mlp": sib}, device_id_type=MESH)
@@ -95,6 +100,7 @@
         return copy
 
     token_float = tok[...].astype(F32)
+    loads["ga"].wait()
     ag1[c, z] = (rms_scale(token_float) * attn_gain[...]).astype(BF16)
     pl.semaphore_wait(barrier, n_z + n_req - 1)
     z_copies = [
@@ -102,6 +108,26 @@
         for k in range(1, n_z)
     ]
     c_copies = [send(ag1.at[c, z], ag1.at[c, z], ss_ag1c.at[0], rs_ag1c.at[0], {"mlp": sib})]
+    for g in range(n_req):
+        at = jnp.int32(0)
+        for t in range(group):
+            if t:
+                at = jnp.where(segments[g, t] == segments[g, t - 1], at + 1, 0)
+            posv[g * group + t:g * group + t + 1, :] = jnp.full((1, HD), at, jnp.int32)
+    extra = 2 * group
+    column = lax.broadcasted_iota(jnp.int32, (group, extra), 1)
+    row_of = lax.broadcasted_iota(jnp.int32, (group, extra), 0)
+    seg_row = jnp.full((group, extra), -1, jnp.int32)
+    for t in range(group):
+        segv[t:t + 1, :] = jnp.full((1, extra), segments[rq, t], jnp.int32)
+        seg_row = jnp.where(column == t, segments[rq, t], seg_row)
+    n_sink = sink_k.shape[0]
+    local = (segv[...] == seg_row) & (column <= row_of)
+    sinks = (column >= group) & (column < group + n_sink)
+    one = jnp.where(local | sinks, 1, 0)
+    emask = jnp.concatenate([one, one], axis=0) > 0
+    block_rows = win_k.shape[0]
+    wpos = owners[rq] * block_rows + lax.broadcasted_iota(jnp.int32, (1, block_rows), 1)
     for k, copy in enumerate(z_copies, 1):
         copy.wait_recv()
         block = ag1.at[c, lax.rem(z + n_z - k, n_z)]
@@ -123,8 +149,9 @@
     loads["k"].wait()
     key_new = jnp.dot(rows, wkey[...], preferred_element_type=F32).astype(BF16)
     loads["v"].wait()
+    for name in ("g", "u", "d"):
+        loads[name].start()
     value_new = jnp.dot(rows, wval[...], preferred_element_type=F32).astype(BF16)
-    n_sink = sink_k.shape[0]
     for target, new, sinks in ((ekf, key_new, sink_k), (evf, value_new, sink_v)):
         target[...] = jnp.zeros_like(target)
         target[0:group, :] = new.astype(F32)
@@ -139,7 +166,7 @@
         pair = jnp.concatenate(
             [own_q[:, (2 * j + i) * HD:(2 * j + i + 1) * HD] for i in range(2)], axis=0)
         scores = lax.dot_general(pair, extra_k[:, lanes], NT, preferred_element_type=F32)
-        weight = jnp.where(emask[...] > 0, weights_of(scores), 0.0)
+        weight = jnp.where(emask, weights_of(scores), 0.0)
         den = jnp.sum(weight, axis=-1, keepdims=True)
         num = jnp.dot(weight.astype(BF16), extra_v[:, lanes], preferred_element_type=F32)
         for i in range(2):
@@ -151,7 +178,9 @@
     for copy in q_copies:
         copy.wait_recv()
     all_q = qbuf[...].reshape(total, q_cols)
-    visible = wpos[...] > pos[...]
+    visible = wpos > posv[:, 0:1]
+    visible = jnp.where(visible, 1, 0)
+    visible = jnp.concatenate([visible, visible], axis=0) > 0
     lane = lax.broadcasted_iota(jnp.int32, (total, HD), 1)
     den_all = jnp.zeros((total, HD), F32)
     for j in range(kv_heads):
@@ -201,32 +230,42 @@
     for k, copy in enumerate(copies, 1):
         copy.wait_recv()
         head_total = head_total + r3[k - 1].astype(F32)
+    for name in ("gpa", "gf", "gpf"):
+        loads[name].wait()
     residual = token_float + rms_scale(head_total) * post_attn_gain[...]
 
-    mine = c * n_req + rq
-    ag2[mine, z] = (rms_scale(residual) * ffn_gain[...]).astype(BF16)
-    copies = [
-        send(ag2.at[mine, z], ag2.at[mine, z], ss_ag2z.at[k], rs_ag2z.at[k], z_peer(k))
+    ag2[0, 0, z] = (rms_scale(residual) * ffn_gain[...]).astype(BF16)
+    z_copies = [
+        send(ag2.at[0, 0, z], ag2.at[0, 0, z], ss_ag2z.at[k], rs_ag2z.at[k], z_peer(k))
         for k in range(1, n_z)
     ]
-    for copy in copies:
-        copy.wait_recv()
-    r_copies = [
-        send(ag2.at[mine], ag2.at[mine], ss_ag2r.at[k], rs_ag2r.at[k], {"req": r_peer(k)})
-        for k in range(1, n_req)
-    ]
-    c_copies = [send(ag2.at[mine], ag2.at[mine], ss_ag2c.at[0], rs_ag2c.at[0], {"mlp": sib})]
-    for k, copy in enumerate(r_copies, 1):
-        copy.wait_recv()
-        block = ag2.at[c * n_req + lax.rem(rq + n_req - k, n_req)]
-        c_copies.append(send(block, block, ss_ag2c.at[k], rs_ag2c.at[k], {"mlp": sib}))
-    for copy in c_copies:
-        copy.wait_recv()
-    for core in range(2):
-        for r in range(n_req):
-            for level in range(n_z):
-                row = r * group + (level * 2 + core) * tp
-                xf[row:row + tp, :] = ag2[core * n_req + r, level].astype(F32)
+    r_copies = {}
+    for step in range(n_z):
+        if step:
+            z_copies[step - 1].wait_recv()
+        level = lax.rem(z + n_z - step, n_z)
+        for k in range(1, n_req):
+            r_copies[step, k] = send(
+                ag2.at[0, 0, level], ag2.at[0, k, level], ss_ag2r.at[step, k],
+                rs_ag2r.at[step, k], {"req": r_peer(k)})
+    c_copies = [send(ag2.at[0, 0], ag2.at[1, 0], ss_ag2c.at[0], rs_ag2c.at[0], {"mlp": sib})]
+    span = n_z * tp
+
+    def unpack(core, k):
+        base = (core * n_req + k) * span
+        for level in range(n_z):
+            xf[base + level * tp:base + (level + 1) * tp, :] = ag2[core, k, level].astype(F32)
+
+    unpack(0, 0)
+    for k in range(1, n_req):
+        for step in range(n_z):
+            r_copies[step, k].wait_recv()
+        c_copies.append(send(
+            ag2.at[0, k], ag2.at[1, k], ss_ag2c.at[k], rs_ag2c.at[k], {"mlp": sib}))
+        unpack(0, k)
+    for k, copy in enumerate(c_copies):
+        copy.wait_recv()
+        unpack(1, k)
     xb[...] = xf[...].astype(BF16)
 
     loads["g"].wait()
@@ -248,52 +287,73 @@
         ffn_hidden(ff - ff % 256, ff % 256)
     loads["d"].wait()
 
-    @pl.loop(0, width // 512)
-    def _(step):
-        lanes = pl.ds(pl.multiple_of(step * 512, 512), 512)
-        acc[:, lanes] = jnp.dot(hid[...], wd[:, lanes], preferred_element_type=F32)
-
-    for core in range(2):
-        for r in range(n_req):
-            for level in range(n_z):
-                row = r * group + (level * 2 + core) * tp
-                t1[core, r, level] = acc[row:row + tp, :].astype(BF16)
-    order = [r_peer(k) for k in list(range(1, n_req)) + [0]]
-    first = [
-        send(t1.at[oc, r], u1.at[r], ss_t1.at[k], rs_t1.at[k], {"mlp": sib})
-        for k, r in enumerate(order)
-    ]
-    second = []
-    for k, r in enumerate(order):
-        first[k].wait_recv()
-        both = t1[c, r].astype(F32) + u1[r].astype(F32)
-        if k < n_req - 1:
-            t2[r] = both.astype(BF16)
-            second.append(send(
-                t2.at[r], u2.at[k], ss_t2.at[k], rs_t2.at[k], {"req": r}))
-    for k, copy in enumerate(second):
-        copy.wait_recv()
-        both = both + u2[k].astype(F32)
-    t3f[...] = both
-    t3[...] = both.astype(BF16)
-    copies = [
-        send(t3.at[lax.rem(z + k, n_z)], u3.at[k - 1], ss_t3.at[k], rs_t3.at[k], z_peer(k))
-        for k in range(1, n_z)
-    ]
-    ffn_out = t3f[z]
-    for k, copy in enumerate(copies, 1):
-        copy.wait_recv()
-        ffn_out = ffn_out + u3[k - 1].astype(F32)
-    out[...] = (residual + rms_scale(ffn_out) * post_ffn_gain[...]).astype(BF16)
+    parts, cols = t1.shape[1], t1.shape[-1]
+    order = list(range(1, n_req)) + [0]
+    first, second, third, kept, finals = {}, {}, {}, {}, {}
+
+    def partial_sums(j):
+        @pl.loop(0, cols // 512)
+        def _(step):
+            start = pl.multiple_of(step * 512, 512)
+            acc[j, :, pl.ds(start, 512)] = jnp.dot(
+                hid[...], wd[:, pl.ds(j * cols + start, 512)], preferred_element_type=F32)
+
+        for core in (1, 0):
+            for k in order:
+                base = (core * n_req + k) * span
+                for level in range(n_z):
+                    row = base + level * tp
+                    t1[core, j, k, level] = acc[j, row:row + tp, :].astype(BF16)
+                if core:
+                    first[j, k] = send(
+                        t1.at[1, j, k], u1.at[j, k], ss_t1.at[j, k], rs_t1.at[j, k], {"mlp": sib})
+
+    def add_cores(j):
+        for k in order:
+            first[j, k].wait_recv()
+            both = t1[0, j, k].astype(F32) + u1[j, k].astype(F32)
+            if k:
+                t2[j, k] = both.astype(BF16)
+                second[j, k] = send(
+                    t2.at[j, k], u2.at[j, k], ss_t2.at[j, k], rs_t2.at[j, k],
+                    {"req": r_peer(n_req - k)})
+            else:
+                t3f[j] = both
+
+    def add_req(j):
+        both = t3f[j]
+        for k in range(1, n_req):
+            second[j, k].wait_recv()
+            both = both + u2[j, k].astype(F32)
+        t3f[j] = both
+        t3[j] = both.astype(BF16)
+        for k in range(1, n_z):
+            third[j, k] = send(
+                t3.at[j, lax.rem(z + k, n_z)], u3.at[j, k], ss_t3.at[j, k], rs_t3.at[j, k],
+                z_peer(k))
+
+    for j in range(parts + 2):
+        if j < parts:
+            partial_sums(j)
+        if 0 <= j - 1 < parts:
+            add_cores(j - 1)
+        if 0 <= j - 2 < parts:
+            add_req(j - 2)
+    squares = jnp.zeros((tp, 1), F32)
+    for j in range(parts):
+        total_j = t3f[j, z]
+        for k in range(1, n_z):
+            third[j, k].wait_recv()
+            total_j = total_j + u3[j, k].astype(F32)
+        finals[j] = total_j
+        squares = squares + jnp.sum(total_j * total_j, axis=-1, keepdims=True)
+    scale = lax.rsqrt(squares / width + EPS)
+    for j in range(parts):
+        lanes = slice(j * cols, (j + 1) * cols)
+        out[:, lanes] = (
+            residual[:, lanes] + finals[j] * scale * post_ffn_gain[:, lanes]).astype(BF16)
     for copy in sent:
         copy.wait_send()
-
-
-def positions(seg_rows):
-    ordering = jnp.arange(seg_rows.shape[-1], dtype=jnp.int32)
-    same_seg = seg_rows[..., :, None] == seg_rows[..., None, :]
-    earlier = ordering[None, :] < ordering[:, None]
-    return jnp.sum((same_seg & earlier).astype(jnp.int32), axis=-1)
 
 
 def shards(
@@ -306,59 +366,52 @@
     n_z = n_mlp // 2
     group = tp * n_mlp
     total = group * n_req
-    block = window_keys.shape[0]
     q_cols, kv_cols, ff = w_query.shape[1], w_key.shape[1], w_gate.shape[0]
-    n_sink = sink_keys.shape[0]
     extra = 2 * group
-    req = lax.axis_index("req")
-    pos = positions(segments).reshape(total, 1)
-    pos = jnp.concatenate([pos, pos], axis=0)
-    owner = jnp.sum(jnp.where(jnp.arange(n_req) == req, owners, 0))
-    wpos = (owner * block + jnp.arange(block, dtype=jnp.int32)).reshape(1, block)
-    seg = lax.dynamic_index_in_dim(segments, req, 0, keepdims=False)
-    order = jnp.arange(group, dtype=jnp.int32)
-    local = (seg[:, None] == seg[None, :]) & (order[None, :] <= order[:, None])
-    sinks = jnp.broadcast_to(jnp.arange(extra - group) < n_sink, (group, extra - group))
-    emask = jnp.concatenate([local, sinks], axis=1).astype(jnp.int32)
-    emask = jnp.concatenate([emask, emask], axis=0)
-
+    parts = 3
+    cols = width // parts
     def v(shape, dtype=BF16):
         return pltpu.VMEM(shape, dtype)
 
     dma = pltpu.SemaphoreType.DMA
     scratch = [v(a.shape) for a in (
         window_keys, window_values, w_query, w_key, w_value, w_out, w_gate, w_up, w_down)]
+    scratch += [v((1, width), F32)] * 4
     scratch += [
-        dma((9,)),
+        dma((13,)),
+        v((total, HD), jnp.int32), v((group, extra), jnp.int32),
         v((2, n_z, tp, width)), v((total, width), F32), v((total, width)),
         v((n_req, group, q_cols)), v((extra, kv_cols), F32), v((extra, kv_cols), F32),
         v((n_req, group, q_cols + HD), F32), v((max(n_req - 1, 1), group, q_cols + HD), F32),
         v((group, width), F32), v((2, n_z, tp, width)), v((n_z, tp, width)),
         v((n_z, tp, width)), v((n_z - 1, tp, width)),
-        v((2 * n_req, n_z, tp, width)), v((total, ff)), v((total, width), F32),
-        v((2, n_req, n_z, tp, width)), v((n_req, n_z, tp, width)),
-        v((n_req, n_z, tp, width)), v((n_req - 1, n_z, tp, width)),
-        v((n_z, tp, width), F32), v((n_z, tp, width)), v((n_z - 1, tp, width)),
+        v((2, n_req, n_z, tp, width)), v((total, ff)), v((parts, total, cols), F32),
+        v((2, parts, n_req, n_z, tp, cols)), v((parts, n_req, n_z, tp, cols)),
+        v((parts, n_req, n_z, tp, cols)), v((parts, n_req, n_z, tp, cols)),
+        v((parts, n_z, tp, cols), F32), v((parts, n_z, tp, cols)), v((parts, n_z, tp, cols)),
         dma((n_z,)), dma((n_z,)), dma((n_z,)), dma((n_z,)),
         dma((n_req,)), dma((n_req,)), dma((n_req,)), dma((n_req,)),
         dma, dma, dma((n_z,)), dma((n_z,)),
-        dma((n_z,)), dma((n_z,)), dma((n_req,)), dma((n_req,)), dma((n_req,)), dma((n_req,)),
-        dma((n_req,)), dma((n_req,)), dma((n_req,)), dma((n_req,)), dma((n_z,)), dma((n_z,)),
+        dma((n_z,)), dma((n_z,)), dma((n_z, n_req)), dma((n_z, n_req)),
+        dma((n_req,)), dma((n_req,)),
+        dma((parts, n_req)), dma((parts, n_req)), dma((parts, n_req)), dma((parts, n_req)),
+        dma((parts, n_z)), dma((parts, n_z)),
     ]
     vmem = pl.BlockSpec(memory_space=pltpu.VMEM)
+    smem = pl.BlockSpec(memory_space=pltpu.SMEM)
     hbm = pl.BlockSpec(memory_space=pl.ANY)
     return pl.pallas_call(
         functools.partial(kernel, n_req, n_mlp),
         name="layer",
         out_shape=jax.ShapeDtypeStruct((tp, width), BF16),
-        in_specs=[vmem] * 10 + [hbm] * 9,
+        in_specs=[vmem, smem, smem, vmem, vmem] + [hbm] * 13,
         out_specs=vmem,
         scratch_shapes=scratch,
         compiler_params=pltpu.CompilerParams(
             collective_id=0, has_side_effects=True, vmem_limit_bytes=62 << 20),
     )(
-        tokens, attn_gain[None], post_attn_gain[None], ffn_gain[None], post_ffn_gain[None],
-        wpos, pos, emask, sink_keys, sink_values,
+        tokens, segments, owners, sink_keys, sink_values,
+        attn_gain, post_attn_gain, ffn_gain, post_ffn_gain,
         window_keys, window_values, w_query, w_key, w_value, w_out, w_gate, w_up, w_down,
     )
 

time: 69.8 us -> 58.4 us (0.84)
  local copies, waits for them, and re-layouts: 8.2 us -> 1.34 us
  other arithmetic: 3.7 us -> 0 us
    broadcast_in_dim x5 -> x0, local copies, waits for them, and re-layouts: 5.36 us -> none  [the longest x1 1.35 us: shards(): attn_gain[None]]
    reduce_sum x2 -> x0, other arithmetic: 2.26 us -> none  [the longest x1 1.29 us: shards(): owner = jnp.sum(jnp.where(jnp.arange(n_req) == req, owners, 0))]
    concatenate x2 -> x0, other arithmetic: 0.75 us -> none  [the longest x1 0.67 us: shards(): emask = jnp.concatenate([emask, emask], axis=0)]
    concatenate x1 -> x0, local copies, waits for them, and re-layouts: 0.73 us -> none  [shards(): pos = jnp.concatenate([pos, pos], axis=0)]
where the time goes in v2:
time: 58.4 us; the launch traced here: 58.2 us
  Pallas kernels  56.9 us (97%)
  local copies, waits for them, and re-layouts  1.34 us (2%)
    pallas_call x1, Pallas kernels, shards(): pl.pallas_call(functools.partial(kernel, n_req, n_mlp), name='layer', out...  56.9 us
    unnamed x1, local copies, waits for them, and re-layouts  1.34 us

profile of v2, /device:TPU:0, one launch (start us, length us, event | category | flops | bytes accessed | tf_op | source)
XLA Modules:
  0.0 58.2 jit_solution(15964845076711728663)
XLA Ops:
  0.0 56.9 %layer.1 = bf16[2,4608]{1,0:T(2,128)(2,1)} custom-call(bf16[2,4608]{1,0:T(2,128)(2,1)} %tok.1, s32[4,16]{1,0:T(4,128)} %segments.1, s32[4]{0:T(128)} %owners.1, bf16[4,256]{1,0:T(4,128)(2,1)} %sink_k.1, bf16[4,256]{1,0:T(4,128)(2,1)} %sink_v.1, f32[4608]{0:T(1024)} %gains_a.1, f32[4608]{0:T(1024)} %gains_pa.1, f32[4608]{0:T(1024)} %gains_f.1, ...), custom_call_target="tpu_custom_call" | custom-call | tf_op jit(solution)/shard_map/layer/pallas_call | solution.py:403
  56.9 1.3 %copy.20 = bf16[2,4608]{1,0:T(2,128)(2,1)} copy(bf16[2,4608]{1,0:T(2,128)(2,1)} %layer.1) | data formatting | bytes 36864

commit v3 on v2

--- a/solution.py
+++ b/solution.py
@@ -78,8 +78,7 @@
         ("g", wg_hbm, wg), ("u", wu_hbm, wu), ("d", wd_hbm, wd),
     )):
         loads[name] = pltpu.make_async_copy(src, dst, load_sem.at[number])
-        if name not in ("g", "u", "d"):
-            loads[name].start()
+        loads[name].start()
 
     barrier = pltpu.get_barrier_semaphore()
     pl.semaphore_signal(barrier, inc=1, device_id={"mlp": sib}, device_id_type=MESH)
@@ -149,8 +148,6 @@
     loads["k"].wait()
     key_new = jnp.dot(rows, wkey[...], preferred_element_type=F32).astype(BF16)
     loads["v"].wait()
-    for name in ("g", "u", "d"):
-        loads[name].start()
     value_new = jnp.dot(rows, wval[...], preferred_element_type=F32).astype(BF16)
     for target, new, sinks in ((ekf, key_new, sink_k), (evf, value_new, sink_v)):
         target[...] = jnp.zeros_like(target)
@@ -368,7 +365,7 @@
     total = group * n_req
     q_cols, kv_cols, ff = w_query.shape[1], w_key.shape[1], w_gate.shape[0]
     extra = 2 * group
-    parts = 3
+    parts = 1
     cols = width // parts
     def v(shape, dtype=BF16):
         return pltpu.VMEM(shape, dtype)

time: 58.4 us -> 57.4 us (0.983)
  Pallas kernels: 56.9 us -> 55.9 us
    pallas_call x1, Pallas kernels: 56.9 us -> 55.9 us  [shards(): pl.pallas_call(functools.partial(kernel, n_req, n_mlp), name='layer', out...]
where the time goes in v3:
time: 57.4 us; the launch traced here: 57.2 us
  Pallas kernels  55.9 us (97%)
  local copies, waits for them, and re-layouts  1.34 us (2%)
    pallas_call x1, Pallas kernels, shards(): pl.pallas_call(functools.partial(kernel, n_req, n_mlp), name='layer', out...  55.9 us
    unnamed x1, local copies, waits for them, and re-layouts  1.34 us

profile of v3, /device:TPU:0, one launch (start us, length us, event | category | flops | bytes accessed | tf_op | source)
XLA Modules:
  0.0 57.2 jit_solution(16942492139913291875)
XLA Ops:
  0.0 55.9 %layer.1 = bf16[2,4608]{1,0:T(2,128)(2,1)} custom-call(bf16[2,4608]{1,0:T(2,128)(2,1)} %tok.1, s32[4,16]{1,0:T(4,128)} %segments.1, s32[4]{0:T(128)} %owners.1, bf16[4,256]{1,0:T(4,128)(2,1)} %sink_k.1, bf16[4,256]{1,0:T(4,128)(2,1)} %sink_v.1, f32[4608]{0:T(1024)} %gains_a.1, f32[4608]{0:T(1024)} %gains_pa.1, f32[4608]{0:T(1024)} %gains_f.1, ...), custom_call_target="tpu_custom_call" | custom-call | tf_op jit(solution)/shard_map/layer/pallas_call | solution.py:400
  55.9 1.3 %copy.20 = bf16[2,4608]{1,0:T(2,128)(2,1)} copy(bf16[2,4608]{1,0:T(2,128)(2,1)} %layer.1) | data formatting | bytes 36864
